TPU v7x, 32 devices: a whole 2x2x4 slice. The times are simulated.
32 devices in a mesh: row: 8 (over z, y), col: 2 (over core), layer: 2 (over x).
Axes of the slice: x: 2, y: 2, z: 4, core: 2. Of those that a mesh axis runs over, the one named last changes fastest.
Arguments:
- matrix: float32 [1, 8, 256, 4, 2, 256], P(None, 'row', None, None, 'col'), may hold values from -8 to 113.137085, as said below
Outputs:
- factored: float32 [1, 8, 256, 4, 2, 256], P(None, 'row', None, 'layer', 'col')
Inputs may be any that keep to these rules, and one draw needn't show every extreme that they name: `matrix`: viewed as in the first step it is symmetric, its leading 2 * 256 x 2 * 256 block is positive definite, and its diagonal entries lie between 2.5 and 5 times the square root of 512.
All inputs are finite; a program needn't handle non-finite values.
Results may differ from a plain program's by a relative error of at most 0.000059.
Values sent between devices are 32-bit elements; how exact they have to be, the bound alone decides.
No kernel may reach another device: no remote copies, remote signals or barrier semaphores. Data moves between devices by JAX's collectives and lax.ppermute only.
A program may use at most 128 MiB of HBM per device.

v0:
```python
import jax
import jax.numpy as jnp
from jax import lax
from jax.sharding import PartitionSpec as P

HIGH = lax.Precision.HIGHEST


def from_root(shard, axis, root):
    mine = lax.axis_index(axis) == root
    return lax.psum(jnp.where(mine, shard, jnp.zeros_like(shard)), axis)


def factor_block(diag_block):
    lower_fac = jnp.linalg.cholesky(diag_block)
    identity = jnp.eye(diag_block.shape[0], dtype=jnp.float32)
    inverse = lax.linalg.triangular_solve(lower_fac, identity, left_side=True, lower=True)
    return (lower_fac, inverse)


def on_device(matrix):
    row_total = lax.axis_size("row")
    col_total = lax.axis_size("col")
    layer_total = lax.axis_size("layer")
    grid_row = lax.axis_index("row")
    grid_col = lax.axis_index("col")
    grid_layer = lax.axis_index("layer")
    row_blocks = matrix.shape[0]
    block_size = matrix.shape[2]
    col_blocks = matrix.shape[3]
    half = block_size // layer_total
    owned = col_blocks // layer_total
    rows = row_blocks * block_size
    tile = matrix.reshape(rows, col_blocks * block_size)
    row_ids = jnp.arange(rows) // block_size * row_total + grid_row
    column = tile[:, :block_size]
    pending = None
    total = None
    panels = []
    for section in range(2):
        diag_block = from_root(column, "row", section % row_total)
        lower_fac, inverse = factor_block(diag_block)
        solved = jnp.dot(column, inverse.T, precision=HIGH, preferred_element_type=jnp.float32)
        repeated = jnp.tile(lower_fac, (row_blocks, 1))
        complete = jnp.where(
            row_ids[:, None] > section,
            solved,
            jnp.where(row_ids[:, None] == section, repeated, 0.0),
        )
        panels.append(complete)
        share = lax.dynamic_slice_in_dim(complete, grid_layer * half, half, 1)
        share = from_root(share, "col", section % col_total)
        gathered = lax.all_gather(
            share.reshape(row_blocks, 1, block_size, half), "row", axis=1, tiled=True
        )
        grouped = gathered.reshape(col_blocks, col_total, block_size, half)
        picked = lax.dynamic_index_in_dim(grouped, grid_col, 1, keepdims=False).reshape(
            col_blocks * block_size, half
        )
        update = lax.dot_general(
            share,
            picked,
            (((1,), (1,)), ((), ())),
            precision=HIGH,
            preferred_element_type=jnp.float32,
        )
        if section == 0:
            head = lax.psum(update[:, :block_size], "layer")
            column = tile[:, :block_size] - head
            pending = update
        else:
            total = pending + update
    reduced = lax.psum_scatter(
        total.reshape(rows, col_blocks, block_size), "layer", scatter_dimension=1, tiled=True
    )
    own_part = (
        lax.dynamic_slice_in_dim(
            tile.reshape(rows, col_blocks, block_size), grid_layer * owned, owned, 1
        )
        - reduced
    )
    replacement = jnp.where(grid_col == 0, panels[0], panels[1])
    global_ids = (grid_layer * owned + jnp.arange(owned)) * col_total + grid_col
    result = jnp.where((global_ids < 2)[None, :, None], replacement[:, None, :], own_part)
    return result.reshape(row_blocks, 1, block_size, owned, 1, block_size)


def solution(mesh):
    in_specs = (P(None, "row", None, None, "col", None),)
    out_specs = P(None, "row", None, "layer", "col", None)
    return jax.shard_map(
        on_device, mesh=mesh, in_specs=in_specs, out_specs=out_specs, check_vma=False
    )
```

profile of v0, /device:TPU:0, one launch (start us, length us, event | category | flops | bytes accessed | tf_op | source)
XLA Modules:
  0.0 472.5 jit_solution(6674159370767984335)
XLA Ops:
  6.5 2.3 copy.16
  9.8 74.7 %all-reduce.7.cloned.1.call-done = f32[256,256]{0,1:T(8,128)} async-done(((f32[256,256]{0,1:T(8,128)}), f32[256,256]{0,1:T(8,128)}) %all-reduce.7.cloned.1.call-update) | async-done | bytes 262160 | tf_op jit(solution)/shard_map/psum | solution.py:11
  85.7 11.7 %cholesky.130 = f32[128,128]{1,0:T(8,128)S(1)} custom-call(f32[128,128]{1,0:T(8,128)S(1)} %cholesky.194), custom_call_target="Cholesky" | custom-call | tf_op jit(solution)/shard_map/jit(cholesky)/cholesky | solution.py:15
  97.4 9.8 %custom-call.13 = f32[1,128,128]{1,2,0:T(8,128)S(1)} custom-call(f32[1,128,128]{2,1,0:T(8,128)S(1)} %get-tuple-element.62), custom_call_target="InvertDiagBlocksLowerTriangular" | custom-call | tf_op jit(solution)/shard_map/jit(cholesky)/cholesky | solution.py:15
  107.7 11.7 %cholesky.147 = f32[128,128]{1,0:T(8,128)S(1)} custom-call(f32[128,128]{1,0:T(8,128)S(1)} %convolution_subtract_fusion.3), custom_call_target="Cholesky" | custom-call | tf_op jit(solution)/shard_map/jit(cholesky)/cholesky | solution.py:15
  122.0 4.8 %while.4 = (s32[]{:T(128)}, f32[256,256]{0,1:T(8,128)S(1)}, s32[2,2]{1,0:T(2,128)S(1)}, f32[2,128,128]{2,1,0:T(8,128)S(1)}, s32[]{:T(128)}) while((s32[]{:T(128)}, f32[256,256]{0,1:T(8,128)S(1)}, s32[2,2]{1,0:T(2,128)S(1)}, f32[2,128,128]{2,1,0:T(8,128)S(1)}, s32[]{:T(128)}) %tuple.46), condition=%wide.while_cond, body=%wide.while_body.sunk | while | flops 2 | bytes 393321 | solution.py:17
  126.8 19.7 %custom-call.14 = f32[2,128,128]{1,2,0:T(8,128)S(1)} custom-call(f32[2,128,128]{2,1,0:T(8,128)S(1)} %get-tuple-element.21), custom_call_target="InvertDiagBlocksLowerTriangular" | custom-call | tf_op jit(solution)/shard_map/triangular_solve/custom-call.0 | solution.py:17
  148.6 17.2 %all-reduce.9.cloned.1.call-done = f32[256,128]{0,1:T(8,128)} async-done(((f32[256,128]{0,1:T(8,128)}), f32[256,128]{0,1:T(8,128)}) %all-reduce.9.cloned.1.call-update) | async-done | bytes 131088 | tf_op jit(solution)/shard_map/psum | solution.py:11
  165.9 42.6 %all-gather.5.cloned.1.call-done = f32[2048,128]{0,1:T(8,128)} async-done(((f32[256,128]{0,1:T(8,128)}), f32[2048,128]{0,1:T(8,128)}) %all-gather.5.cloned.1.call-update) | async-done | bytes 1048592 | tf_op jit(solution)/shard_map/all_gather | solution.py:53
  208.5 2.1 reshape.86
  210.6 1.6 dynamic-slice_reduce_fusion.1
  215.1 22.4 %all-reduce.11.cloned.1.call-done = f32[256,256]{0,1:T(8,128)} async-done(((f32[256,256]{0,1:T(8,128)}), f32[256,256]{0,1:T(8,128)}) %all-reduce.11.cloned.1.call-update) | async-done | bytes 262160 | tf_op jit(solution)/shard_map/psum | solution.py:68
  237.5 1.7 broadcast_select_fusion
  239.5 72.3 %all-reduce.13.cloned.1.call-done = f32[256,256]{0,1:T(8,128)} async-done(((f32[256,256]{0,1:T(8,128)}), f32[256,256]{0,1:T(8,128)}) %all-reduce.13.cloned.1.call-update) | async-done | bytes 262160 | tf_op jit(solution)/shard_map/psum | solution.py:11
  313.0 11.7 %cholesky.164 = f32[128,128]{1,0:T(8,128)S(1)} custom-call(f32[128,128]{1,0:T(8,128)S(1)} %cholesky.197), custom_call_target="Cholesky" | custom-call | tf_op jit(solution)/shard_map/jit(cholesky)/cholesky | solution.py:15
  324.8 9.8 %custom-call.15 = f32[1,128,128]{1,2,0:T(8,128)S(1)} custom-call(f32[1,128,128]{2,1,0:T(8,128)S(1)} %get-tuple-element.60), custom_call_target="InvertDiagBlocksLowerTriangular" | custom-call | tf_op jit(solution)/shard_map/jit(cholesky)/cholesky | solution.py:15
  335.1 11.7 %cholesky.181 = f32[128,128]{1,0:T(8,128)S(1)} custom-call(f32[128,128]{1,0:T(8,128)S(1)} %convolution_subtract_fusion.2), custom_call_target="Cholesky" | custom-call | tf_op jit(solution)/shard_map/jit(cholesky)/cholesky | solution.py:15
  349.8 4.4 while.5
  354.2 19.7 %custom-call.16 = f32[2,128,128]{1,2,0:T(8,128)S(1)} custom-call(f32[2,128,128]{2,1,0:T(8,128)S(1)} %get-tuple-element.22), custom_call_target="InvertDiagBlocksLowerTriangular" | custom-call | tf_op jit(solution)/shard_map/triangular_solve/custom-call.0 | solution.py:17
  376.7 17.2 %all-reduce.15.cloned.1.call-done = f32[256,128]{0,1:T(8,128)} async-done(((f32[256,128]{0,1:T(8,128)}), f32[256,128]{0,1:T(8,128)}) %all-reduce.15.cloned.1.call-update) | async-done | bytes 131088 | tf_op jit(solution)/shard_map/psum | solution.py:11
  393.9 42.6 %all-gather.7.cloned.1.call-done = f32[2048,128]{0,1:T(8,128)} async-done(((f32[256,128]{0,1:T(8,128)}), f32[2048,128]{0,1:T(8,128)}) %all-gather.7.cloned.1.call-update) | async-done | bytes 1048592 | tf_op jit(solution)/shard_map/all_gather | solution.py:53
  436.6 2.1 reshape.89
  438.7 1.6 dynamic-slice_reduce_fusion
  445.0 17.9 %reduce-scatter.2.cloned.1.call-done = f32[256,2,256]{2,0,1:T(8,128)} async-done(((f32[256,4,256]{2,0,1:T(8,128)}), f32[256,2,256]{2,0,1:T(8,128)}) %reduce-scatter.2.cloned.1.call-update) | async-done | bytes 524304 | tf_op jit(solution)/shard_map/reduce_scatter | solution.py:73
  (109 shorter events, 30.6 us)
Async XLA Ops:
  6.5 77.9 %all-reduce.7.cloned.1.call-start = ((), (), s32[]{:S(2)}) async-start(), calls=%async_computation.1 | async-start | bytes 524288 | tf_op jit(solution)/shard_map/psum | solution.py:11
  9.6 156.2 %all-reduce.9.cloned.1.call-start = ((), (), s32[]{:S(2)}) async-start(), calls=%async_computation.2 | async-start | bytes 262144 | tf_op jit(solution)/shard_map/psum | solution.py:11
  84.4 1.2 copy-start.1
  148.5 60.0 %all-gather.5.cloned.1.call-start = ((), (), s32[]{:S(2)}) async-start(), calls=%async_computation.7 | async-start | bytes 1179648 | tf_op jit(solution)/shard_map/all_gather | solution.py:53
  165.8 71.7 %all-reduce.11.cloned.1.call-start = ((), (), s32[]{:S(2)}) async-start(), calls=%async_computation.3 | async-start | bytes 524288 | tf_op jit(solution)/shard_map/psum | solution.py:68
  212.2 0.9 copy-start.4
  215.0 96.7 %all-reduce.13.cloned.1.call-start = ((), (), s32[]{:S(2)}) async-start(), calls=%async_computation.4 | async-start | bytes 524288 | tf_op jit(solution)/shard_map/psum | solution.py:11
  239.2 154.7 %all-reduce.15.cloned.1.call-start = ((), (), s32[]{:S(2)}) async-start(), calls=%async_computation.5 | async-start | bytes 262144 | tf_op jit(solution)/shard_map/psum | solution.py:11
  311.8 1.2 copy-start.2
  374.6 1.0 copy-start.3
  376.6 59.9 %all-gather.7.cloned.1.call-start = ((), (), s32[]{:S(2)}) async-start(), calls=%async_computation.8 | async-start | bytes 1179648 | tf_op jit(solution)/shard_map/all_gather | solution.py:53
  393.9 69.0 %reduce-scatter.2.cloned.1.call-start = ((), (), s32[]{:S(2)}) async-start(), calls=%async_computation.6 | async-start | bytes 1572864 | tf_op jit(solution)/shard_map/reduce_scatter | solution.py:73
  440.3 0.9 copy-start.5
  443.3 1.2 copy-start
Sparse Core Ops, SparseCore 0:
  10.7 73.7 all-reduce.6
  148.7 17.0 all-reduce.8
  167.8 40.5 all-gather.4
  215.2 22.2 all-reduce.10
  240.7 71.0 all-reduce.12
  376.7 17.0 all-reduce.14
  395.9 40.5 all-gather.6
  443.5 19.3 reduce-scatter.1
where the time goes:
time: 481 us; the launch traced here: 472 us
  waiting for transfers between devices  307 us (64%)
  other arithmetic  113 us (23%)
  local copies, waits for them, and re-layouts  28.5 us (6%)
  between operations  16.8 us (3%)
  matrix products  5.65 us (1%)
    psum x4, waiting for transfers between devices, from_root(): return lax.psum(jnp.where(mine, shard, jnp.zeros_like(shard)), axis)  181 us
    all_gather x2, waiting for transfers between devices, on_device(): lax.all_gather(share.reshape(row_blocks, 1, block_size, half), 'row', axi...  85.2 us
    another operation x13, other arithmetic, factor_block(): lower_fac = jnp.linalg.cholesky(diag_block)  68.7 us
    another operation x5, other arithmetic, factor_block(): lax.linalg.triangular_solve(lower_fac, identity, left_side=True, lower=True)  39.4 us
    psum x1, waiting for transfers between devices, on_device(): head = lax.psum(update[:, :block_size], 'layer')  22.4 us
    reduce_scatter x1, waiting for transfers between devices, on_device(): lax.psum_scatter(total.reshape(rows, col_blocks, block_size), 'layer', sc...  17.9 us
  transfers between devices with their start and end apart: 8, of which 8 were waited for; matrix products, arithmetic and copies ran while one was open for 0% of the time, Pallas kernels for 0%

commit v1 on v0

--- a/solution.py
+++ b/solution.py
@@ -4,6 +4,30 @@
 from jax.sharding import PartitionSpec as P
 
 HIGH = lax.Precision.HIGHEST
+
+
+def track_the_zone(z_in, join_dim):
+    carry_in = list(z_in.shape[1:])
+    carry_in[join_dim] *= z_in.shape[0]
+    return jnp.moveaxis(z_in, 0, join_dim).reshape(carry_in)
+
+
+def _report_spots(x_local, axis_key):
+    parts_n = lax.axis_size(axis_key)
+    earlier = x_local[None]
+    for b in range(parts_n.bit_length() - 1):
+        y2 = 1 << b
+        after = lax.ppermute(earlier, axis_key, list(map(lambda it: (it, it ^ y2), range(parts_n))))
+        current_arr = jnp.stack([earlier, after], axis=0)
+        arr_out = lax.axis_index(axis_key) >> b & 1
+        earlier = jnp.where(arr_out == 0, current_arr, current_arr[::-1]).reshape(
+            -1, *x_local.shape
+        )
+    return earlier
+
+
+def deliver_slots(t0, view, out_dim):
+    return track_the_zone(_report_spots(t0, view), out_dim)
 
 
 def from_root(shard, axis, root):
@@ -50,9 +74,7 @@
         panels.append(complete)
         share = lax.dynamic_slice_in_dim(complete, grid_layer * half, half, 1)
         share = from_root(share, "col", section % col_total)
-        gathered = lax.all_gather(
-            share.reshape(row_blocks, 1, block_size, half), "row", axis=1, tiled=True
-        )
+        gathered = deliver_slots(share.reshape(row_blocks, 1, block_size, half), "row", 1)
         grouped = gathered.reshape(col_blocks, col_total, block_size, half)
         picked = lax.dynamic_index_in_dim(grouped, grid_col, 1, keepdims=False).reshape(
             col_blocks * block_size, half

time: 481 us -> 465 us (0.967); the launches traced: 472 us -> 464 us
  waiting for transfers between devices: 307 us -> 290 us
  starting transfers between devices: 0.46 us -> 12.8 us
  local copies, waits for them, and re-layouts: 28.5 us -> 21.6 us
    all_gather x2 -> x0, waiting for transfers between devices: 85.2 us -> none  [on_device(): lax.all_gather(share.reshape(row_blocks, 1, block_size, half), 'row', axi...]
    ppermute x0 -> x6, waiting for transfers between devices: none -> 63.6 us  [_report_spots(): lax.ppermute(earlier, axis_key, list(map(lambda it: (it, it ^ y2), range(...]
    ppermute x0 -> x6, starting transfers between devices: none -> 12.6 us  [_report_spots(): lax.ppermute(earlier, axis_key, list(map(lambda it: (it, it ^ y2), range(...]
  transfers between devices with their start and end apart: 8 -> 12, of which waited for: 8 -> 12; matrix products, arithmetic and copies ran while one was open for 0% -> 0% of each run, Pallas kernels for 0% -> 0%
where the time goes in v1:
time: 465 us; the launch traced here: 464 us
  waiting for transfers between devices  290 us (62%)
  other arithmetic  117 us (25%)
  local copies, waits for them, and re-layouts  21.6 us (5%)
  between operations  16.5 us (4%)
  starting transfers between devices  12.8 us (3%)
  matrix products  5.66 us (1%)
    psum x4, waiting for transfers between devices, from_root(): return lax.psum(jnp.where(mine, shard, jnp.zeros_like(shard)), axis)  182 us
    another operation x13, other arithmetic, factor_block(): lower_fac = jnp.linalg.cholesky(diag_block)  68.6 us
    ppermute x6, waiting for transfers between devices, _report_spots(): lax.ppermute(earlier, axis_key, list(map(lambda it: (it, it ^ y2), range(...  63.6 us
    another operation x5, other arithmetic, factor_block(): lax.linalg.triangular_solve(lower_fac, identity, left_side=True, lower=True)  39.4 us
    psum x1, waiting for transfers between devices, on_device(): head = lax.psum(update[:, :block_size], 'layer')  24.5 us
    reduce_scatter x1, waiting for transfers between devices, on_device(): lax.psum_scatter(total.reshape(rows, col_blocks, block_size), 'layer', sc...  19.9 us
    ppermute x6, starting transfers between devices, _report_spots(): lax.ppermute(earlier, axis_key, list(map(lambda it: (it, it ^ y2), range(...  12.6 us
  transfers between devices with their start and end apart: 12, of which 12 were waited for; matrix products, arithmetic and copies ran while one was open for 0% of the time, Pallas kernels for 0%

profile of v1, /device:TPU:0, one launch (start us, length us, event | category | flops | bytes accessed | tf_op | source)
XLA Modules:
  0.0 464.4 jit_solution(6509699208277848412)
XLA Ops:
  9.8 74.7 %all-reduce.7.cloned.1.call-done = f32[256,256]{0,1:T(8,128)} async-done(((f32[256,256]{0,1:T(8,128)}), f32[256,256]{0,1:T(8,128)}) %all-reduce.7.cloned.1.call-update) | async-done | bytes 262160 | tf_op jit(solution)/shard_map/psum | solution.py:35
  85.7 11.7 %cholesky.130 = f32[128,128]{1,0:T(8,128)S(1)} custom-call(f32[128,128]{1,0:T(8,128)S(1)} %cholesky.194), custom_call_target="Cholesky" | custom-call | tf_op jit(solution)/shard_map/jit(cholesky)/cholesky | solution.py:39
  97.4 9.8 %custom-call.13 = f32[1,128,128]{1,2,0:T(8,128)S(1)} custom-call(f32[1,128,128]{2,1,0:T(8,128)S(1)} %get-tuple-element.82), custom_call_target="InvertDiagBlocksLowerTriangular" | custom-call | tf_op jit(solution)/shard_map/jit(cholesky)/cholesky | solution.py:39
  107.7 11.7 %cholesky.147 = f32[128,128]{1,0:T(8,128)S(1)} custom-call(f32[128,128]{1,0:T(8,128)S(1)} %convolution_subtract_fusion.3), custom_call_target="Cholesky" | custom-call | tf_op jit(solution)/shard_map/jit(cholesky)/cholesky | solution.py:39
  121.8 4.2 while.4
  126.0 19.7 %custom-call.14 = f32[2,128,128]{1,2,0:T(8,128)S(1)} custom-call(f32[2,128,128]{2,1,0:T(8,128)S(1)} %get-tuple-element.21), custom_call_target="InvertDiagBlocksLowerTriangular" | custom-call | tf_op jit(solution)/shard_map/triangular_solve/custom-call.0 | solution.py:41
  147.8 17.2 %all-reduce.9.cloned.1.call-done = f32[256,128]{0,1:T(8,128)} async-done(((f32[256,128]{0,1:T(8,128)}), f32[256,128]{0,1:T(8,128)}) %all-reduce.9.cloned.1.call-update) | async-done | bytes 131088 | tf_op jit(solution)/shard_map/psum | solution.py:35
  166.8 4.1 collective-permute-done
  173.7 5.9 %collective-permute-done.1 = f32[2,1,1,256,128]{3,4,0,2,1:T(8,128)S(1)} collective-permute-done((f32[2,1,1,256,128]{3,4,0,2,1:T(8,128)S(1)}, f32[2,1,1,256,128]{3,4,0,2,1:T(8,128)S(1)}, u32[]{:S(2)}, u32[]{:S(2)}) %collective-permute-start.1) | collective-permute-done | bytes 262176 | tf_op jit(solution)/shard_map/ppermute | solution.py:20
  179.9 2.7 collective-permute-start.2
  182.8 21.8 %collective-permute-done.2 = f32[4,1,1,256,128]{4,3,0,2,1:T(8,128)} collective-permute-done((f32[4,1,1,256,128]{4,3,0,2,1:T(8,128)S(1)}, f32[4,1,1,256,128]{4,3,0,2,1:T(8,128)}, u32[]{:S(2)}, u32[]{:S(2)}) %collective-permute-start.2) | collective-permute-done | bytes 524320 | tf_op jit(solution)/shard_map/ppermute | solution.py:20
  208.7 24.5 %all-reduce.11.cloned.1.call-done = f32[256,256]{0,1:T(8,128)} async-done(((f32[256,256]{0,1:T(8,128)}), f32[256,256]{0,1:T(8,128)}) %all-reduce.11.cloned.1.call-update) | async-done | bytes 262160 | tf_op jit(solution)/shard_map/psum | solution.py:90
  235.0 72.5 %all-reduce.13.cloned.1.call-done = f32[256,256]{0,1:T(8,128)} async-done(((f32[256,256]{0,1:T(8,128)}), f32[256,256]{0,1:T(8,128)}) %all-reduce.13.cloned.1.call-update) | async-done | bytes 262160 | tf_op jit(solution)/shard_map/psum | solution.py:35
  308.7 11.7 %cholesky.164 = f32[128,128]{1,0:T(8,128)S(1)} custom-call(f32[128,128]{1,0:T(8,128)S(1)} %cholesky.197), custom_call_target="Cholesky" | custom-call | tf_op jit(solution)/shard_map/jit(cholesky)/cholesky | solution.py:39
  320.4 9.8 %custom-call.15 = f32[1,128,128]{1,2,0:T(8,128)S(1)} custom-call(f32[1,128,128]{2,1,0:T(8,128)S(1)} %get-tuple-element.80), custom_call_target="InvertDiagBlocksLowerTriangular" | custom-call | tf_op jit(solution)/shard_map/jit(cholesky)/cholesky | solution.py:39
  330.7 11.7 %cholesky.181 = f32[128,128]{1,0:T(8,128)S(1)} custom-call(f32[128,128]{1,0:T(8,128)S(1)} %convolution_subtract_fusion.2), custom_call_target="Cholesky" | custom-call | tf_op jit(solution)/shard_map/jit(cholesky)/cholesky | solution.py:39
  345.5 4.4 while.5
  349.9 19.7 %custom-call.16 = f32[2,128,128]{1,2,0:T(8,128)S(1)} custom-call(f32[2,128,128]{2,1,0:T(8,128)S(1)} %get-tuple-element.22), custom_call_target="InvertDiagBlocksLowerTriangular" | custom-call | tf_op jit(solution)/shard_map/triangular_solve/custom-call.0 | solution.py:41
  372.4 17.2 %all-reduce.15.cloned.1.call-done = f32[256,128]{0,1:T(8,128)} async-done(((f32[256,128]{0,1:T(8,128)}), f32[256,128]{0,1:T(8,128)}) %all-reduce.15.cloned.1.call-update) | async-done | bytes 131088 | tf_op jit(solution)/shard_map/psum | solution.py:35
  391.3 4.1 collective-permute-done.3
  398.3 5.9 %collective-permute-done.4 = f32[2,1,1,256,128]{3,4,0,2,1:T(8,128)S(1)} collective-permute-done((f32[2,1,1,256,128]{3,4,0,2,1:T(8,128)S(1)}, f32[2,1,1,256,128]{3,4,0,2,1:T(8,128)S(1)}, u32[]{:S(2)}, u32[]{:S(2)}) %collective-permute-start.4) | collective-permute-done | bytes 262176 | tf_op jit(solution)/shard_map/ppermute | solution.py:20
  404.4 2.7 collective-permute-start.5
  407.3 21.8 %collective-permute-done.5 = f32[4,1,1,256,128]{4,3,0,2,1:T(8,128)} collective-permute-done((f32[4,1,1,256,128]{4,3,0,2,1:T(8,128)S(1)}, f32[4,1,1,256,128]{4,3,0,2,1:T(8,128)}, u32[]{:S(2)}, u32[]{:S(2)}) %collective-permute-start.5) | collective-permute-done | bytes 524320 | tf_op jit(solution)/shard_map/ppermute | solution.py:20
  435.1 19.9 %reduce-scatter.2.cloned.1.call-done = f32[256,2,256]{2,0,1:T(8,128)} async-done(((f32[256,4,256]{2,0,1:T(8,128)}), f32[256,2,256]{2,0,1:T(8,128)}) %reduce-scatter.2.cloned.1.call-update) | async-done | bytes 524304 | tf_op jit(solution)/shard_map/reduce_scatter | solution.py:95
  (127 shorter events, 46.4 us)
Async XLA Ops:
  6.5 77.9 %all-reduce.7.cloned.1.call-start = ((), (), s32[]{:S(2)}) async-start(), calls=%async_computation.1 | async-start | bytes 524288 | tf_op jit(solution)/shard_map/psum | solution.py:35
  9.6 155.4 %all-reduce.9.cloned.1.call-start = ((), (), s32[]{:S(2)}) async-start(), calls=%async_computation.2 | async-start | bytes 262144 | tf_op jit(solution)/shard_map/psum | solution.py:35
  84.4 1.2 copy-start.1
  147.8 85.4 %all-reduce.11.cloned.1.call-start = ((), (), s32[]{:S(2)}) async-start(), calls=%async_computation.3 | async-start | bytes 524288 | tf_op jit(solution)/shard_map/psum | solution.py:90
  165.0 5.9 %collective-permute-start = (f32[1,1,1,256,128]{3,4,2,1,0:T(8,128)}, f32[1,1,1,256,128]{3,4,2,1,0:T(8,128)S(1)}, u32[]{:S(2)}, u32[]{:S(2)}) collective-permute-start(f32[1,1,1,256,128]{3,4,2,1,0:T(8,128)} %bitcast.127), channel_id=1, source_target_pairs={{0,4},{4,0},{8,12},{12,8},{16,20},{20,16},{24,28},{28,24},{1,5},{5... | collective-permute-start | bytes 393224 | tf_op jit(solution)/shard_map/ppermute | solution.py:20
  171.9 7.7 %collective-permute-start.1 = (f32[2,1,1,256,128]{3,4,0,2,1:T(8,128)S(1)}, f32[2,1,1,256,128]{3,4,0,2,1:T(8,128)S(1)}, u32[]{:S(2)}, u32[]{:S(2)}) collective-permute-start(f32[2,1,1,256,128]{3,4,0,2,1:T(8,128)S(1)} %get-tuple-element.78), channel_id=1, source_target_pairs={{0,8},{4,12},{8,0},{12,4},{16,24},{20,28},{24,16},{28,20},{1,9},{5... | collective-permute-start | bytes 786440 | tf_op jit(solution)/shard_map/ppermute | solution.py:20
  179.9 24.7 %collective-permute-start.2 = (f32[4,1,1,256,128]{4,3,0,2,1:T(8,128)S(1)}, f32[4,1,1,256,128]{4,3,0,2,1:T(8,128)}, u32[]{:S(2)}, u32[]{:S(2)}) collective-permute-start(f32[4,1,1,256,128]{4,3,0,2,1:T(8,128)S(1)} %copy.61), channel_id=1, source_target_pairs={{0,16},{4,20},{8,24},{12,28},{16,0},{20,4},{24,8},{28,12},{1,17},{... | collective-permute-start | bytes 1572872 | tf_op jit(solution)/shard_map/ppermute | solution.py:20
  205.8 0.9 copy-start.4
  208.6 98.8 %all-reduce.13.cloned.1.call-start = ((), (), s32[]{:S(2)}) async-start(), calls=%async_computation.4 | async-start | bytes 524288 | tf_op jit(solution)/shard_map/psum | solution.py:35
  234.9 154.7 %all-reduce.15.cloned.1.call-start = ((), (), s32[]{:S(2)}) async-start(), calls=%async_computation.5 | async-start | bytes 262144 | tf_op jit(solution)/shard_map/psum | solution.py:35
  307.5 1.2 copy-start.2
  370.2 1.0 copy-start.3
  372.3 82.7 %reduce-scatter.2.cloned.1.call-start = ((), (), s32[]{:S(2)}) async-start(), calls=%async_computation.6 | async-start | bytes 1572864 | tf_op jit(solution)/shard_map/reduce_scatter | solution.py:95
  389.6 5.9 %collective-permute-start.3 = (f32[1,1,1,256,128]{3,4,2,1,0:T(8,128)}, f32[1,1,1,256,128]{3,4,2,1,0:T(8,128)S(1)}, u32[]{:S(2)}, u32[]{:S(2)}) collective-permute-start(f32[1,1,1,256,128]{3,4,2,1,0:T(8,128)} %bitcast.129), channel_id=1, source_target_pairs={{0,4},{4,0},{8,12},{12,8},{16,20},{20,16},{24,28},{28,24},{1,5},{5... | collective-permute-start | bytes 393224 | tf_op jit(solution)/shard_map/ppermute | solution.py:20
  396.4 7.7 %collective-permute-start.4 = (f32[2,1,1,256,128]{3,4,0,2,1:T(8,128)S(1)}, f32[2,1,1,256,128]{3,4,0,2,1:T(8,128)S(1)}, u32[]{:S(2)}, u32[]{:S(2)}) collective-permute-start(f32[2,1,1,256,128]{3,4,0,2,1:T(8,128)S(1)} %get-tuple-element.76), channel_id=1, source_target_pairs={{0,8},{4,12},{8,0},{12,4},{16,24},{20,28},{24,16},{28,20},{1,9},{5... | collective-permute-start | bytes 786440 | tf_op jit(solution)/shard_map/ppermute | solution.py:20
  404.4 24.7 %collective-permute-start.5 = (f32[4,1,1,256,128]{4,3,0,2,1:T(8,128)S(1)}, f32[4,1,1,256,128]{4,3,0,2,1:T(8,128)}, u32[]{:S(2)}, u32[]{:S(2)}) collective-permute-start(f32[4,1,1,256,128]{4,3,0,2,1:T(8,128)S(1)} %copy.73), channel_id=1, source_target_pairs={{0,16},{4,20},{8,24},{12,28},{16,0},{20,4},{24,8},{28,12},{1,17},{... | collective-permute-start | bytes 1572872 | tf_op jit(solution)/shard_map/ppermute | solution.py:20
  430.3 0.9 copy-start.5
  433.4 1.2 copy-start
Sparse Core Ops, SparseCore 0:
  10.7 73.7 all-reduce.6
  147.9 17.0 all-reduce.8
  208.8 24.3 all-reduce.10
  236.4 71.0 all-reduce.12
  372.4 17.0 all-reduce.14
  433.5 21.4 reduce-scatter.1
